TPU v7x, 256 devices: a whole 4x4x8 slice. The times are simulated.
256 devices in a mesh: row: 8 (over y, core), col: 32 (over x, z).
Axes of the slice: x: 4, y: 4, z: 8, core: 2. Of those that a mesh axis runs over, the one named last changes fastest.
Arguments:
- object_field: float32 [2, 2048, 8192], P(None, 'row', 'col'), may hold values from -6 to 6
- probe_field: float32 [2, 2, 128, 128], replicated, may hold values from -6 to 6
- amplitudes: float32 [8, 32, 24, 128, 128], P('row', 'col'), may hold values from 0.3 to 6
- offsets: int32 [8, 32, 24, 2], P('row', 'col'), may hold values from -64 to 191
- counts: int32 [8, 32], P('row', 'col'), may hold values from 1 to 24, as said below
Outputs:
- object_next: float32 [2, 2048, 8192], P(None, 'row', 'col')
- probe_next: float32 [2, 2, 128, 128], replicated
Inputs may be any that keep to these rules, and one draw needn't show every extreme that they name: `counts`: slots at and above a tile's count are unused; some tile has all 24 slots live.
All inputs are finite; a program needn't handle non-finite values.
Results may differ from a plain program's by a relative error of at most 0.0001.
Values sent between devices are 32-bit elements; how exact they have to be, the bound alone decides.
A program may use at most 64 MiB of HBM per device.

v0:
```python
import functools

import jax
import jax.numpy as jnp
import ml_dtypes
import numpy as np
from jax import lax
from jax.experimental import pallas as pl
from jax.experimental.pallas import tpu as pltpu
from jax.sharding import PartitionSpec as P

F32 = jnp.float32
BF16 = jnp.bfloat16
EPSILON = 1e-06
MESH = pl.DeviceIdType.MESH
VMEM = pl.BlockSpec(memory_space=pltpu.VMEM)
SMEM = pl.BlockSpec(memory_space=pltpu.SMEM)

SIZE = 128
TILE = 256
HALF = 64
EXT = TILE + 2 * HALF
ROWS, COLS = 8, 32
XS, YS, ZS = 4, 4, 8
UNROLL = 4

DIRS = [(-1, 0), (1, 0), (0, -1), (0, 1), (-1, -1), (-1, 1), (1, -1), (1, 1)]


def dft_tables():
    k = np.arange(SIZE)
    angles = 2 * np.pi / SIZE * ((k[:, None] * k[None, :]) % SIZE)
    c, s = np.cos(angles) / np.sqrt(SIZE), np.sin(angles) / np.sqrt(SIZE)
    terms = []
    for table in (np.block([[c, -s], [s, c]]), np.block([[c, s], [-s, c]])):
        high = table.astype(ml_dtypes.bfloat16)
        low = (table - high.astype(np.float64)).astype(ml_dtypes.bfloat16)
        terms += [high, low]
    return np.stack(terms)


def half_turn(x):
    return pltpu.roll(x, HALF, 1)


def lanes(rows):
    return lax.broadcasted_iota(jnp.int32, (rows, SIZE), 1)


def neighbour(direction):
    row = lax.axis_index("row") + direction[0]
    col = lax.axis_index("col") + direction[1]
    valid = (row >= 0) & (row < ROWS) & (col >= 0) & (col < COLS)
    return (row, col), valid


def signal_neighbours(barrier):
    count = jnp.int32(0)
    for direction in DIRS:
        where, valid = neighbour(direction)

        @pl.when(valid)
        def _():
            pl.semaphore_signal(barrier, 1, device_id=where, device_id_type=MESH)

        count = count + valid.astype(jnp.int32)
    return count


class Exchange:
    def __init__(self, dsts, send, recv):
        self.dsts, self.send, self.recv = dsts, send, recv

    def copy(self, k, src, where):
        return pltpu.make_async_remote_copy(
            src, self.dsts[k], self.send.at[k], self.recv.at[k], device_id=where, device_id_type=MESH
        )

    def start(self, k, src):
        where, valid = neighbour(DIRS[k])

        @pl.when(valid)
        def _():
            self.copy(k, src, where).start()

    def clear_missing(self):
        for k, (dr, dc) in enumerate(DIRS):
            _, valid = neighbour((-dr, -dc))

            @pl.when(jnp.logical_not(valid))
            def _():
                self.dsts[k][...] = jnp.zeros_like(self.dsts[k])

    def wait_recv(self, k):
        where, valid = neighbour((-DIRS[k][0], -DIRS[k][1]))

        @pl.when(valid)
        def _():
            self.copy(k, self.dsts[k], where).wait_recv()

    def wait_send(self, k, src):
        where, valid = neighbour(DIRS[k])

        @pl.when(valid)
        def _():
            self.copy(k, src, where).wait_send()


def exchange_scratch(vertical, side, corner):
    shapes = [vertical] * 2 + [side] * 2 + [corner] * 4
    return [pltpu.VMEM(shape, F32) for shape in shapes] + [pltpu.SemaphoreType.DMA((8,))] * 2


FIELD_SCRATCH = exchange_scratch((2, 2, HALF, SIZE), (TILE, SIZE), (HALF, SIZE))
WEIGHT_SCRATCH = exchange_scratch((2, HALF, SIZE), (TILE // 2, SIZE), (HALF, SIZE))


def as_exchange(refs):
    return Exchange(refs[:8], refs[8], refs[9])


def send_margins(exchange, own, left, right):
    lane = lanes(TILE)
    left[...] = jnp.where(lane < HALF, own[0, 0], half_turn(own[1, 0]))
    right[...] = jnp.where(lane >= HALF, own[0, 1], half_turn(own[1, 1]))
    low, high = pl.ds(0, HALF), pl.ds(TILE - HALF, HALF)
    srcs = [
        own.at[:, :, low, :], own.at[:, :, high, :], left, right,
        left.at[low], right.at[low], left.at[high], right.at[high],
    ]
    for k in (2, 3, 4, 5, 6, 7, 0, 1):
        exchange.start(k, srcs[k])
    return srcs


def fill_extended(exchange, ext):
    for k in range(8):
        exchange.wait_recv(k)
    bufs = exchange.dsts
    low, mid, high = pl.ds(0, HALF), pl.ds(HALF, TILE), pl.ds(HALF + TILE, HALF)
    ext[:, 1:3, high, :] = bufs[0][...]
    ext[:, 1:3, low, :] = bufs[1][...]
    for panel, rows, buf in (
        (3, mid, bufs[2]), (0, mid, bufs[3]),
        (3, high, bufs[4]), (0, high, bufs[5]), (3, low, bufs[6]), (0, low, bufs[7]),
    ):
        ext[0, panel, rows, :] = buf[...]
        ext[1, panel, rows, :] = half_turn(buf[...])


def send_totals(exchange, tot, left, right):
    lane = lanes(EXT)
    left[...] = jnp.where(lane >= HALF, tot[0, 0], half_turn(tot[1, 0]))
    right[...] = jnp.where(lane < HALF, tot[0, 3], half_turn(tot[1, 3]))
    low, mid, high = pl.ds(0, HALF), pl.ds(HALF, TILE), pl.ds(HALF + TILE, HALF)
    srcs = [
        tot.at[:, 1:3, low, :], tot.at[:, 1:3, high, :], left.at[mid], right.at[mid],
        left.at[low], right.at[low], left.at[high], right.at[high],
    ]
    for k in (2, 3, 4, 5, 6, 7, 0, 1):
        exchange.start(k, srcs[k])
    return srcs


def send_weights(exchange, wgt, left, right):
    lane = lanes(SIZE)
    first, second = pl.ds(HALF, SIZE), pl.ds(HALF + SIZE, SIZE)
    left[...] = jnp.where(lane >= HALF, wgt[0, first, :], half_turn(wgt[0, second, :]))
    right[...] = jnp.where(lane < HALF, wgt[3, first, :], half_turn(wgt[3, second, :]))
    low, high = pl.ds(0, HALF), pl.ds(HALF + TILE, HALF)
    srcs = [
        wgt.at[1:3, low, :], wgt.at[1:3, high, :], left, right,
        wgt.at[0, low, :], wgt.at[3, low, :], wgt.at[0, high, :], wgt.at[3, high, :],
    ]
    for k in (2, 3, 4, 5, 6, 7, 0, 1):
        exchange.start(k, srcs[k])
    return srcs


def with_corners(side, below, above):
    return jnp.concatenate(
        [side[:HALF] + above, side[HALF : TILE - HALF], side[TILE - HALF :] + below], axis=0
    )


def with_vertical(centre, below, above):
    return jnp.concatenate(
        [centre[:HALF] + above, centre[HALF : TILE - HALF], centre[TILE - HALF :] + below], axis=0
    )


def gathered_totals(exchange, tot):
    for k in range(8):
        exchange.wait_recv(k)
    bufs = exchange.dsts
    lane = lanes(TILE)
    right = with_corners(bufs[2][...], bufs[4][...], bufs[6][...])
    left = with_corners(bufs[3][...], bufs[5][...], bufs[7][...])
    rights = (right, half_turn(right))
    lefts = (left, half_turn(left))
    parts = []
    for part in range(2):
        panels = []
        for panel in range(2):
            centre = tot[part, 1 + panel, pl.ds(HALF, TILE), :]
            centre = with_vertical(centre, bufs[0][part, panel], bufs[1][part, panel])
            extra = jnp.where(lane < HALF, lefts[part], 0.0) if panel == 0 else jnp.where(lane >= HALF, rights[part], 0.0)
            panels.append(centre + extra)
        parts.append(panels)
    return parts


def gathered_weights(exchange, wgt):
    for k in range(8):
        exchange.wait_recv(k)
    bufs = exchange.dsts
    lane = lanes(TILE)
    right = jnp.concatenate([bufs[2][...], half_turn(bufs[2][...])], axis=0)
    left = jnp.concatenate([bufs[3][...], half_turn(bufs[3][...])], axis=0)
    right = with_corners(right, bufs[4][...], bufs[6][...])
    left = with_corners(left, bufs[5][...], bufs[7][...])
    panels = []
    for panel in range(2):
        centre = with_vertical(wgt[1 + panel, pl.ds(HALF, TILE), :], bufs[0][panel], bufs[1][panel])
        extra = jnp.where(lane < HALF, left, 0.0) if panel == 0 else jnp.where(lane >= HALF, right, 0.0)
        panels.append(centre + extra)
    return panels


def margins_kernel(field, ext, *refs):
    exchange, (own, left, right) = as_exchange(refs[:10]), refs[10:]
    barrier = pltpu.get_barrier_semaphore()
    count = signal_neighbours(barrier)
    exchange.clear_missing()
    for part in range(2):
        for panel in range(2):
            value = field[part, :, panel * SIZE : (panel + 1) * SIZE]
            own[part, panel] = value
            ext[part, 1 + panel, pl.ds(HALF, TILE), :] = value
    pl.semaphore_wait(barrier, count)
    srcs = send_margins(exchange, own, left, right)
    fill_extended(exchange, ext)
    for k in range(8):
        exchange.wait_send(k, srcs[k])


def middle_kernel(tot, wgt, ext, probe, new_ext, den, *refs):
    totals, weights, margins = (as_exchange(refs[i : i + 10]) for i in (0, 10, 20))
    tot_left, tot_right, wgt_left, wgt_right, own, left, right = refs[30:]
    barrier = pltpu.get_barrier_semaphore()
    count = signal_neighbours(barrier)
    for exchange in (totals, weights, margins):
        exchange.clear_missing()
    pl.semaphore_wait(barrier, count)
    tot_srcs = send_totals(totals, tot, tot_left, tot_right)
    wgt_srcs = send_weights(weights, wgt, wgt_left, wgt_right)
    power = probe[0, 0] ** 2 + probe[0, 1] ** 2 + probe[1, 0] ** 2 + probe[1, 1] ** 2
    regular = 0.1 * jnp.max(jnp.max(power, axis=0, keepdims=True), axis=1, keepdims=True) + EPSILON
    numer = gathered_totals(totals, tot)
    weight = gathered_weights(weights, wgt)
    centre = pl.ds(HALF, TILE)
    for panel in range(2):
        divisor = weight[panel] + regular
        den[panel] = divisor
        for part in range(2):
            value = (numer[part][panel] + regular * ext[part, 1 + panel, centre, :]) / divisor
            own[part, panel] = value
            new_ext[part, 1 + panel, centre, :] = value
    srcs = send_margins(margins, own, left, right)
    fill_extended(margins, new_ext)
    for k in range(8):
        totals.wait_send(k, tot_srcs[k])
        weights.wait_send(k, wgt_srcs[k])
        margins.wait_send(k, srcs[k])


SHARE = 4 * SIZE // (2 * XS * YS)


def last_kernel(tot, den, ext, probe, grad_a, grad_b, field, probe_new, *refs):
    totals = as_exchange(refs[:10])
    (tot_left, tot_right, total, from_core, half, from_plane, piece, from_line, fresh,
     core_send, core_recv, plane_send, plane_recv, line_send, line_recv,
     spread_send, spread_recv, back_send, back_recv) = refs[10:]
    row, col = lax.axis_index("row"), lax.axis_index("col")
    y, core = row // 2, row % 2
    x, z = col // ZS, col % ZS
    place = x * YS + y

    def in_plane(d):
        other = (place + d) % (XS * YS)
        return other, ((other % YS) * 2 + core, (other // YS) * ZS + z)

    def in_line(d):
        other = (z + d) % ZS
        return other, (row, x * ZS + other)

    partner = (y * 2 + (1 - core), col)
    barrier = pltpu.get_barrier_semaphore()
    count = signal_neighbours(barrier)
    pl.semaphore_signal(barrier, 1, device_id=partner, device_id_type=MESH)
    for d in range(1, XS * YS):
        pl.semaphore_signal(barrier, 1, device_id=in_plane(d)[1], device_id_type=MESH)
    for d in range(1, ZS):
        pl.semaphore_signal(barrier, 1, device_id=in_line(d)[1], device_id_type=MESH)
    totals.clear_missing()
    for part in range(2):
        for mode in range(2):
            rows = pl.ds((part * 2 + mode) * SIZE, SIZE)
            total[rows, :] = grad_a[part, mode] + grad_b[part, mode]
    pl.semaphore_wait(barrier, count + 1 + (XS * YS - 1) + (ZS - 1))

    def remote(src, dst, send, recv, where):
        return pltpu.make_async_remote_copy(src, dst, send, recv, device_id=where, device_id_type=MESH)

    middle = 2 * SIZE
    mine = pl.multiple_of(core * middle, middle)
    theirs = pl.multiple_of((1 - core) * middle, middle)
    swap = remote(total.at[pl.ds(theirs, middle)], from_core, core_send, core_recv, partner)
    swap.start()
    tot_srcs = send_totals(totals, tot, tot_left, tot_right)
    swap.wait_recv()
    half[...] = total[pl.ds(mine, middle), :] + from_core[...]

    def plane_copy(d):
        other, where = in_plane(d)
        rows = pl.ds(pl.multiple_of(other * SHARE, SHARE), SHARE)
        return remote(half.at[rows], from_plane.at[d], plane_send.at[d], plane_recv.at[d], where)

    for d in range(1, XS * YS):
        plane_copy(d).start()

    numer = gathered_totals(totals, tot)
    power = probe[0:SIZE] ** 2
    for k in range(1, 4):
        power = power + probe[k * SIZE : (k + 1) * SIZE] ** 2
    regular = 0.1 * jnp.max(jnp.max(power, axis=0, keepdims=True), axis=1, keepdims=True) + EPSILON
    for part in range(2):
        for panel in range(2):
            own = ext[part, 1 + panel, pl.ds(HALF, TILE), :]
            field[part, :, panel * SIZE : (panel + 1) * SIZE] = (numer[part][panel] + regular * own) / den[panel]

    share = half[pl.ds(pl.multiple_of(place * SHARE, SHARE), SHARE), :]
    for d in range(1, XS * YS):
        plane_copy(d).wait_recv()
        share = share + from_plane[d]
    piece[...] = share
    from_line[z] = share

    def line_copy(d):
        _, where = in_line(d)
        return remote(piece, from_line.at[z], line_send.at[d], line_recv.at[d], where)

    def line_arrival(d):
        source = (z - d + ZS) % ZS
        return remote(piece, from_line.at[source], line_send.at[d], line_recv.at[d], in_line(d)[1])

    for d in range(1, ZS):
        line_copy(d).start()
    for d in range(1, ZS):
        line_arrival(d).wait_recv()
    summed = from_line[0]
    for k in range(1, ZS):
        summed = summed + from_line[k]
    rows = pl.ds(pl.multiple_of(mine + place * SHARE, SHARE), SHARE)
    slots = float(ROWS * COLS * 24)
    fresh[rows, :] = probe[rows, :] + summed / slots

    def spread_copy(d):
        _, where = in_plane(d)
        return remote(fresh.at[rows], fresh.at[rows], spread_send.at[d], spread_recv.at[d], where)

    def spread_arrival(d):
        source = (place - d + XS * YS) % (XS * YS)
        there = pl.ds(pl.multiple_of(mine + source * SHARE, SHARE), SHARE)
        return remote(fresh.at[rows], fresh.at[there], spread_send.at[d], spread_recv.at[d], in_plane(d)[1])

    for d in range(1, XS * YS):
        spread_copy(d).start()
    for d in range(1, XS * YS):
        spread_arrival(d).wait_recv()
    back = remote(fresh.at[pl.ds(mine, middle)], fresh.at[pl.ds(mine, middle)], back_send, back_recv, partner)
    back.start()
    arrival = remote(fresh.at[pl.ds(theirs, middle)], fresh.at[pl.ds(theirs, middle)], back_send, back_recv, partner)
    arrival.wait_recv()
    probe_new[...] = fresh[...]
    swap.wait_send()
    back.wait_send()
    for d in range(1, XS * YS):
        plane_copy(d).wait_send()
        spread_copy(d).wait_send()
    for d in range(1, ZS):
        line_copy(d).wait_send()
    for k in range(8):
        totals.wait_send(k, tot_srcs[k])


def split(x):
    high = x.astype(BF16)
    return high, (x - high.astype(F32)).astype(BF16)


def dot(a, b):
    return jnp.dot(a, b, preferred_element_type=F32)


def on_rows(table, which, x):
    high, low = split(x)
    big, small = table[2 * which], table[2 * which + 1]
    return dot(big, high) + dot(big, low) + dot(small, high)


def on_columns(x, table, which):
    high, low = split(x)
    big, small = table[2 * which], table[2 * which + 1]
    return dot(high, big) + dot(low, big) + dot(high, small)


def visit_kernel(with_weight, off, cnt, ext, probe, table, amp, *refs):
    if with_weight:
        tot, wgt, grad, spread = refs
        wgt[...] = jnp.zeros_like(wgt)
    else:
        tot, grad, spread = refs
    tot[...] = jnp.zeros_like(tot)
    grad[...] = jnp.zeros_like(grad)
    spread[...] = jnp.zeros_like(spread)
    count = cnt[0]
    lane = lanes(SIZE)

    def step(index, carry):
        modes = [(probe[0, m], probe[1, m]) for m in range(2)]
        power = modes[0][0] ** 2 + modes[0][1] ** 2 + modes[1][0] ** 2 + modes[1][1] ** 2
        exits, states = [], []
        for u in range(UNROLL):
            slot = index * UNROLL + u
            row = off[slot, 0] + HALF
            col = off[slot, 1] + SIZE
            panel, shift = col // SIZE, col % SIZE
            live = (slot < count).astype(F32)
            upper = lane >= shift
            back = (SIZE - shift) % SIZE
            window = []
            for part in range(2):
                first = ext[part, panel, pl.ds(row, SIZE), :]
                second = ext[part, panel + 1, pl.ds(row, SIZE), :]
                window.append(pltpu.roll(jnp.where(upper, first, second), back, 1))
            squared = window[0] * window[0] + window[1] * window[1]
            mean = jnp.sum(jnp.sum(squared, axis=0, keepdims=True), axis=1, keepdims=True) * (1.0 / SIZE**2) + EPSILON
            scale = live / mean
            spread[...] += squared * scale
            real = jnp.concatenate([pr * window[0] - pi * window[1] for pr, pi in modes], axis=1)
            imag = jnp.concatenate([pr * window[1] + pi * window[0] for pr, pi in modes], axis=1)
            exits.append(jnp.concatenate([real, imag], axis=0))
            states.append((slot, row, panel, shift, upper, live, window[0] * scale, window[1] * scale))
        first = [on_rows(table, 1, x) for x in exits]
        turned = jnp.concatenate(
            [
                jnp.concatenate([y[:SIZE, m * SIZE : (m + 1) * SIZE], y[SIZE:, m * SIZE : (m + 1) * SIZE]], axis=1)
                for y in first
                for m in range(2)
            ],
            axis=0,
        )
        spectrum = on_columns(turned, table, 0)
        scaled = []
        for u in range(UNROLL):
            z = spectrum[u * 2 * SIZE : (u + 1) * 2 * SIZE]
            sq = z * z
            level = sq[:SIZE, :SIZE] + sq[:SIZE, SIZE:] + sq[SIZE:, :SIZE] + sq[SIZE:, SIZE:]
            factor = amp[states[u][0]] * jnp.minimum(lax.rsqrt(level), 1.0)
            both = jnp.concatenate([factor, factor], axis=1)
            scaled += [z[:SIZE] * both, z[SIZE:] * both]
        middle = on_columns(jnp.concatenate(scaled, axis=0), table, 1)
        terms = [[0.0, 0.0], [0.0, 0.0]]
        for u in range(UNROLL):
            slot, row, panel, shift, upper, live, wr, wi = states[u]
            q = middle[u * 2 * SIZE : (u + 1) * 2 * SIZE]
            revised = on_rows(
                table,
                0,
                jnp.concatenate(
                    [
                        jnp.concatenate([q[:SIZE, :SIZE], q[SIZE:, :SIZE]], axis=1),
                        jnp.concatenate([q[:SIZE, SIZE:], q[SIZE:, SIZE:]], axis=1),
                    ],
                    axis=0,
                ),
            )
            real, imag = 0.0, 0.0
            for m in range(2):
                vr = revised[:SIZE, m * SIZE : (m + 1) * SIZE]
                vi = revised[SIZE:, m * SIZE : (m + 1) * SIZE]
                pr, pi = modes[m]
                real = real + (pr * vr + pi * vi)
                imag = imag + (pr * vi - pi * vr)
                terms[m][0] = terms[m][0] + (wr * vr + wi * vi)
                terms[m][1] = terms[m][1] + (wr * vi - wi * vr)
            places = [(tot.at[0], real), (tot.at[1], imag)]
            if with_weight:
                places.append((wgt, power))
            for ref, value in places:
                moved = pltpu.roll(value * live, shift, 1)
                ref[panel, pl.ds(row, SIZE), :] += jnp.where(upper, moved, 0.0)
                ref[panel + 1, pl.ds(row, SIZE), :] += jnp.where(upper, 0.0, moved)
        for m in range(2):
            for part in range(2):
                grad[part, m] += terms[m][part]
        return carry

    lax.fori_loop(0, (count + UNROLL - 1) // UNROLL, step, 0)
    for part in range(2):
        for m in range(2):
            grad[part, m] -= probe[part, m] * spread[...]


def shape(*dims):
    return jax.ShapeDtypeStruct(dims, F32)


def visit(with_weight, off, cnt, ext, probe, table, amp):
    outs = [shape(2, 4, EXT, SIZE)] + [shape(4, EXT, SIZE)] * with_weight + [shape(2, 2, SIZE, SIZE)]
    return pl.pallas_call(
        functools.partial(visit_kernel, with_weight),
        out_shape=outs,
        in_specs=[SMEM, SMEM, VMEM, VMEM, VMEM, VMEM],
        out_specs=[VMEM] * len(outs),
        scratch_shapes=[pltpu.VMEM((SIZE, SIZE), F32)],
        compiler_params=pltpu.CompilerParams(vmem_limit_bytes=32 << 20),
        name="visit",
    )(off, cnt, ext, probe, table, amp)


def remote_call(kernel, name, collective_id, outs, scratch, *args):
    return pl.pallas_call(
        kernel,
        out_shape=outs,
        in_specs=[VMEM] * len(args),
        out_specs=jax.tree.map(lambda _: VMEM, outs),
        scratch_shapes=scratch,
        compiler_params=pltpu.CompilerParams(
            collective_id=collective_id, has_side_effects=True, vmem_limit_bytes=32 << 20
        ),
        name=name,
    )(*args)


def local(field, probe, amplitudes, offsets, counts):
    amp = amplitudes[0, 0]
    off = offsets[0, 0]
    cnt = counts[0]
    table = jnp.asarray(dft_tables())
    buffer = pltpu.VMEM((TILE, SIZE), F32)
    long = pltpu.VMEM((EXT, SIZE), F32)
    own = pltpu.VMEM((2, 2, TILE, SIZE), F32)
    ext = remote_call(
        margins_kernel, "margins", 0, shape(2, 4, EXT, SIZE), FIELD_SCRATCH + [own, buffer, buffer], field
    )
    tot, wgt, grad_a = visit(True, off, cnt, ext, probe, table, amp)
    packed = pltpu.VMEM((SIZE, SIZE), F32)
    ext, den = remote_call(
        middle_kernel, "middle", 1, [shape(2, 4, EXT, SIZE), shape(2, TILE, SIZE)],
        FIELD_SCRATCH + WEIGHT_SCRATCH + FIELD_SCRATCH + [long, long, packed, packed, own, buffer, buffer],
        tot, wgt, ext, probe,
    )
    tot, grad_b = visit(False, off, cnt, ext, probe, table, amp)
    plane, line = XS * YS, ZS
    dma = pltpu.SemaphoreType.DMA
    scratch = FIELD_SCRATCH + [
        long, long,
        pltpu.VMEM((4 * SIZE, SIZE), F32),
        pltpu.VMEM((2 * SIZE, SIZE), F32),
        pltpu.VMEM((2 * SIZE, SIZE), F32),
        pltpu.VMEM((plane, SHARE, SIZE), F32),
        pltpu.VMEM((SHARE, SIZE), F32),
        pltpu.VMEM((line, SHARE, SIZE), F32),
        pltpu.VMEM((4 * SIZE, SIZE), F32),
        dma, dma, dma((plane,)), dma((plane,)), dma((line,)), dma((line,)), dma((plane,)), dma((plane,)), dma, dma,
    ]
    field_new, probe_new = remote_call(
        last_kernel, "last", 2, [shape(2, TILE, TILE), shape(4 * SIZE, SIZE)], scratch,
        tot, den, ext, probe.reshape(4 * SIZE, SIZE), grad_a, grad_b,
    )
    return field_new, probe_new.reshape(2, 2, SIZE, SIZE)


def solution(mesh):
    in_specs = (
        P(None, "row", "col"),
        P(),
        P("row", "col", None, None, None),
        P("row", "col", None, None),
        P("row", "col"),
    )
    out_specs = (P(None, "row", "col"), P())
    return jax.shard_map(local, mesh=mesh, in_specs=in_specs, out_specs=out_specs, check_vma=False)
```

profile of v0, /device:TPU:1, one launch (start us, length us, event | category | flops | bytes accessed | tf_op | source)
XLA Modules:
  0.0 99.1 jit_solution(7775491359066748319)
XLA Ops:
  0.6 0.0 copy-start.1
  0.6 0.0 copy-start
  1.4 0.8 copy.9.off
  2.2 0.0 copy-start.4
  2.2 1.0 %copy-done.4 = f32[2,256,256]{2,1,0:T(8,128)S(1)} copy-done((f32[2,256,256]{2,1,0:T(8,128)S(1)}, f32[2,256,256]{2,1,0:T(8,128)}, u32[]{:S(2)}) %copy-start.4) | copy-done | bytes 524312
  3.2 10.7 %margins.1.ext = f32[2,4,384,128]{3,2,1,0:T(8,128)S(1)} custom-call(f32[2,256,256]{2,1,0:T(8,128)S(1)} %copy-done.4), custom_call_target="tpu_custom_call" | custom-call | tf_op jit(solution)/shard_map/margins/pallas_call | solution.py:535
  14.0 0.0 copy-done.1
  14.0 0.0 copy-done
  14.0 0.0 copy-start.2
  14.0 1.0 %copy-done.2 = bf16[4,256,256]{2,1,0:T(8,128)(2,1)S(1)} copy-done((bf16[4,256,256]{2,1,0:T(8,128)(2,1)S(1)}, bf16[4,256,256]{2,1,0:T(8,128)(2,1)}, u32[]{:S(2)}) %copy-start.2) | copy-done | bytes 524312
  15.0 7.0 %visit.2 = (f32[2,4,384,128]{3,2,1,0:T(8,128)S(1)}, f32[4,384,128]{2,1,0:T(8,128)S(1)}, f32[2,2,128,128]{3,2,1,0:T(8,128)S(1)}) custom-call(s32[24,2]{1,0:T(8,128)S(1)} %copy.9.off, s32[1]{0:T(128)} %bitcast.5.cnt, f32[2,4,384,128]{3,2,1,0:T(8,128)S(1)} %margins.1.ext, f32[2,2,128,128]{3,2,1,0:T(8,128)S(1)} %copy-done.1, bf16[4,256,256]{2,1,0:T(8,128)(2,1)S(1)} %copy-done.2, ...), custom_call_target="tpu_custom_call" | custom-call | tf_op jit(solution)/shard_map/visit/pallas_call | solution.py:523
  22.0 0.0 copy-start.3
  22.0 21.2 %middle.1 = (f32[2,4,384,128]{3,2,1,0:T(8,128)S(1)}, f32[2,256,128]{2,1,0:T(8,128)S(1)}) custom-call(f32[2,4,384,128]{3,2,1,0:T(8,128)S(1)} %get-tuple-element.11.tot, f32[4,384,128]{2,1,0:T(8,128)S(1)} %get-tuple-element.12.wgt, f32[2,4,384,128]{3,2,1,0:T(8,128)S(1)} %margins.1.ext, f32[2,2,128,128]{3,2,1,0:T(8,128)S(1)} %copy-done.1), custom_call_target="tpu_custom_call" | custom-call | tf_op jit(solution)/shard_map/middle/pallas_call | solution.py:535
  43.2 0.0 copy-done.3
  43.2 7.0 %visit.3 = (f32[2,4,384,128]{3,2,1,0:T(8,128)S(1)}, f32[2,2,128,128]{3,2,1,0:T(8,128)S(1)}) custom-call(s32[24,2]{1,0:T(8,128)S(1)} %copy.9.off, s32[1]{0:T(128)} %bitcast.6.cnt, f32[2,4,384,128]{3,2,1,0:T(8,128)S(1)} %get-tuple-element.13.ext, f32[2,2,128,128]{3,2,1,0:T(8,128)S(1)} %copy-done.1, bf16[4,256,256]{2,1,0:T(8,128)(2,1)S(1)} %copy-done.3, ...), custom_call_target="tpu_custom_call" | custom-call | tf_op jit(solution)/shard_map/visit/pallas_call | solution.py:523
  50.2 47.4 %last.1 = (f32[2,256,256]{2,1,0:T(8,128)S(1)}, f32[512,128]{1,0:T(8,128)S(1)}) custom-call(f32[2,4,384,128]{3,2,1,0:T(8,128)S(1)} %get-tuple-element.14.tot, f32[2,256,128]{2,1,0:T(8,128)S(1)} %get-tuple-element.15.den, f32[2,4,384,128]{3,2,1,0:T(8,128)S(1)} %get-tuple-element.13.ext, f32[512,128]{1,0:T(8,128)S(1)} %bitcast.9, ...), custom_call_target="tpu_custom_call" | custom-call | tf_op jit(solution)/shard_map/last/pallas_call | solution.py:535
  97.6 0.8 copy.13
  98.3 0.7 copy.14
Async XLA Ops:
  0.6 13.3 %copy-start.1 = (f32[2,2,128,128]{3,2,1,0:T(8,128)S(1)}, f32[2,2,128,128]{3,2,1,0:T(8,128)}, u32[]{:S(2)}) copy-start(f32[2,2,128,128]{3,2,1,0:T(8,128)} %probe.5) | copy-start | bytes 786436
  0.6 13.3 %copy-start = (f32[1,1,24,128,128]{4,3,2,1,0:T(8,128)S(1)}, f32[1,1,24,128,128]{4,3,2,1,0:T(8,128)}, u32[]{:S(2)}) copy-start(f32[1,1,24,128,128]{4,3,2,1,0:T(8,128)} %param.8) | copy-start | bytes 4718596
  2.2 1.0 %copy-start.4 = (f32[2,256,256]{2,1,0:T(8,128)S(1)}, f32[2,256,256]{2,1,0:T(8,128)}, u32[]{:S(2)}) copy-start(f32[2,256,256]{2,1,0:T(8,128)} %field.1) | copy-start | bytes 1572868
  14.0 1.0 %copy-start.2 = (bf16[4,256,256]{2,1,0:T(8,128)(2,1)S(1)}, bf16[4,256,256]{2,1,0:T(8,128)(2,1)}, u32[]{:S(2)}) copy-start(bf16[4,256,256]{2,1,0:T(8,128)(2,1)} %constant.2.clone.table) | copy-start | bytes 1572868
  22.0 21.2 %copy-start.3 = (bf16[4,256,256]{2,1,0:T(8,128)(2,1)S(1)}, bf16[4,256,256]{2,1,0:T(8,128)(2,1)}, u32[]{:S(2)}) copy-start(bf16[4,256,256]{2,1,0:T(8,128)(2,1)} %constant.2.clone.table) | copy-start | bytes 1572868
where the time goes:
time: 98.1 us; the launch traced here: 99.1 us
  Pallas kernels  93.2 us (95%)
  local copies, waits for them, and re-layouts  4.35 us (4%)
  between operations  1.5 us (2%)
    pallas_call x3, Pallas kernels, remote_call(): pl.pallas_call(kernel, out_shape=outs, in_specs=[VMEM] * len(args), out_s...  79.3 us
    pallas_call x2, Pallas kernels, visit(): pl.pallas_call(functools.partial(visit_kernel, with_weight), out_shape=ou...  13.9 us
    unnamed x12, local copies, waits for them, and re-layouts  3.59 us

commit v1 on v0

--- a/solution.py
+++ b/solution.py
@@ -22,7 +22,7 @@
 EXT = TILE + 2 * HALF
 ROWS, COLS = 8, 32
 XS, YS, ZS = 4, 4, 8
-UNROLL = 4
+PAIR = 2
 
 DIRS = [(-1, 0), (1, 0), (0, -1), (0, 1), (-1, -1), (-1, 1), (1, -1), (1, 1)]
 
@@ -119,10 +119,13 @@
     return Exchange(refs[:8], refs[8], refs[9])
 
 
-def send_margins(exchange, own, left, right):
+def pack_margins(own, left, right):
     lane = lanes(TILE)
     left[...] = jnp.where(lane < HALF, own[0, 0], half_turn(own[1, 0]))
     right[...] = jnp.where(lane >= HALF, own[0, 1], half_turn(own[1, 1]))
+
+
+def send_margins(exchange, own, left, right):
     low, high = pl.ds(0, HALF), pl.ds(TILE - HALF, HALF)
     srcs = [
         own.at[:, :, low, :], own.at[:, :, high, :], left, right,
@@ -148,10 +151,13 @@
         ext[1, panel, rows, :] = half_turn(buf[...])
 
 
-def send_totals(exchange, tot, left, right):
+def pack_totals(tot, left, right):
     lane = lanes(EXT)
     left[...] = jnp.where(lane >= HALF, tot[0, 0], half_turn(tot[1, 0]))
     right[...] = jnp.where(lane < HALF, tot[0, 3], half_turn(tot[1, 3]))
+
+
+def send_totals(exchange, tot, left, right):
     low, mid, high = pl.ds(0, HALF), pl.ds(HALF, TILE), pl.ds(HALF + TILE, HALF)
     srcs = [
         tot.at[:, 1:3, low, :], tot.at[:, 1:3, high, :], left.at[mid], right.at[mid],
@@ -162,11 +168,14 @@
     return srcs
 
 
-def send_weights(exchange, wgt, left, right):
+def pack_weights(wgt, left, right):
     lane = lanes(SIZE)
     first, second = pl.ds(HALF, SIZE), pl.ds(HALF + SIZE, SIZE)
     left[...] = jnp.where(lane >= HALF, wgt[0, first, :], half_turn(wgt[0, second, :]))
     right[...] = jnp.where(lane < HALF, wgt[3, first, :], half_turn(wgt[3, second, :]))
+
+
+def send_weights(exchange, wgt, left, right):
     low, high = pl.ds(0, HALF), pl.ds(HALF + TILE, HALF)
     srcs = [
         wgt.at[1:3, low, :], wgt.at[1:3, high, :], left, right,
@@ -228,17 +237,24 @@
 
 
 def margins_kernel(field, ext, *refs):
-    exchange, (own, left, right) = as_exchange(refs[:10]), refs[10:]
+    exchange, (own, left, right, arrived) = as_exchange(refs[:10]), refs[10:]
+    loads = []
+    for part in range(2):
+        for panel in range(2):
+            src = field.at[part, :, pl.ds(panel * SIZE, SIZE)]
+            loads.append(pltpu.make_async_copy(src, own.at[part, panel], arrived.at[part * 2 + panel]))
+            loads[-1].start()
     barrier = pltpu.get_barrier_semaphore()
     count = signal_neighbours(barrier)
     exchange.clear_missing()
+    for load in loads:
+        load.wait()
+    pack_margins(own, left, right)
+    pl.semaphore_wait(barrier, count)
+    srcs = send_margins(exchange, own, left, right)
     for part in range(2):
         for panel in range(2):
-            value = field[part, :, panel * SIZE : (panel + 1) * SIZE]
-            own[part, panel] = value
-            ext[part, 1 + panel, pl.ds(HALF, TILE), :] = value
-    pl.semaphore_wait(barrier, count)
-    srcs = send_margins(exchange, own, left, right)
+            ext[part, 1 + panel, pl.ds(HALF, TILE), :] = own[part, panel]
     fill_extended(exchange, ext)
     for k in range(8):
         exchange.wait_send(k, srcs[k])
@@ -251,6 +267,8 @@
     count = signal_neighbours(barrier)
     for exchange in (totals, weights, margins):
         exchange.clear_missing()
+    pack_totals(tot, tot_left, tot_right)
+    pack_weights(wgt, wgt_left, wgt_right)
     pl.semaphore_wait(barrier, count)
     tot_srcs = send_totals(totals, tot, tot_left, tot_right)
     wgt_srcs = send_weights(weights, wgt, wgt_left, wgt_right)
@@ -266,6 +284,7 @@
             value = (numer[part][panel] + regular * ext[part, 1 + panel, centre, :]) / divisor
             own[part, panel] = value
             new_ext[part, 1 + panel, centre, :] = value
+    pack_margins(own, left, right)
     srcs = send_margins(margins, own, left, right)
     fill_extended(margins, new_ext)
     for k in range(8):
@@ -308,6 +327,7 @@
         for mode in range(2):
             rows = pl.ds((part * 2 + mode) * SIZE, SIZE)
             total[rows, :] = grad_a[part, mode] + grad_b[part, mode]
+    pack_totals(tot, tot_left, tot_right)
     pl.semaphore_wait(barrier, count + 1 + (XS * YS - 1) + (ZS - 1))
 
     def remote(src, dst, send, recv, where):
@@ -316,19 +336,28 @@
     middle = 2 * SIZE
     mine = pl.multiple_of(core * middle, middle)
     theirs = pl.multiple_of((1 - core) * middle, middle)
-    swap = remote(total.at[pl.ds(theirs, middle)], from_core, core_send, core_recv, partner)
-    swap.start()
+
+    def share_of(start, d):
+        other, _ = in_plane(d)
+        return pl.ds(pl.multiple_of(start + other * SHARE, SHARE), SHARE)
+
+    def swap_copy(d):
+        return remote(total.at[share_of(theirs, d)], from_core.at[share_of(0, d)], core_send.at[d], core_recv.at[d], partner)
+
+    order = list(range(1, XS * YS)) + [0]
+    for d in order:
+        swap_copy(d).start()
     tot_srcs = send_totals(totals, tot, tot_left, tot_right)
-    swap.wait_recv()
-    half[...] = total[pl.ds(mine, middle), :] + from_core[...]
 
     def plane_copy(d):
-        other, where = in_plane(d)
-        rows = pl.ds(pl.multiple_of(other * SHARE, SHARE), SHARE)
-        return remote(half.at[rows], from_plane.at[d], plane_send.at[d], plane_recv.at[d], where)
-
-    for d in range(1, XS * YS):
-        plane_copy(d).start()
+        _, where = in_plane(d)
+        return remote(half.at[share_of(0, d)], from_plane.at[d], plane_send.at[d], plane_recv.at[d], where)
+
+    for d in order:
+        swap_copy(d).wait_recv()
+        half[share_of(0, d), :] = total[share_of(mine, d), :] + from_core[share_of(0, d), :]
+        if d:
+            plane_copy(d).start()
 
     numer = gathered_totals(totals, tot)
     power = probe[0:SIZE] ** 2
@@ -375,17 +404,22 @@
         there = pl.ds(pl.multiple_of(mine + source * SHARE, SHARE), SHARE)
         return remote(fresh.at[rows], fresh.at[there], spread_send.at[d], spread_recv.at[d], in_plane(d)[1])
 
+    def back_copy(d, start):
+        there = pl.ds(pl.multiple_of(start + (place - d + XS * YS) % (XS * YS) * SHARE, SHARE), SHARE)
+        return remote(fresh.at[there], fresh.at[there], back_send.at[d], back_recv.at[d], partner)
+
     for d in range(1, XS * YS):
         spread_copy(d).start()
+    back_copy(0, mine).start()
     for d in range(1, XS * YS):
         spread_arrival(d).wait_recv()
-    back = remote(fresh.at[pl.ds(mine, middle)], fresh.at[pl.ds(mine, middle)], back_send, back_recv, partner)
-    back.start()
-    arrival = remote(fresh.at[pl.ds(theirs, middle)], fresh.at[pl.ds(theirs, middle)], back_send, back_recv, partner)
-    arrival.wait_recv()
+        back_copy(d, mine).start()
+    for d in range(XS * YS):
+        back_copy(d, theirs).wait_recv()
     probe_new[...] = fresh[...]
-    swap.wait_send()
-    back.wait_send()
+    for d in range(XS * YS):
+        swap_copy(d).wait_send()
+        back_copy(d, mine).wait_send()
     for d in range(1, XS * YS):
         plane_copy(d).wait_send()
         spread_copy(d).wait_send()
@@ -400,115 +434,204 @@
     return high, (x - high.astype(F32)).astype(BF16)
 
 
-def dot(a, b):
-    return jnp.dot(a, b, preferred_element_type=F32)
-
-
-def on_rows(table, which, x):
-    high, low = split(x)
-    big, small = table[2 * which], table[2 * which + 1]
-    return dot(big, high) + dot(big, low) + dot(small, high)
-
-
-def on_columns(x, table, which):
-    high, low = split(x)
-    big, small = table[2 * which], table[2 * which + 1]
-    return dot(high, big) + dot(low, big) + dot(high, small)
-
-
-def visit_kernel(with_weight, off, cnt, ext, probe, table, amp, *refs):
+def turned(y):
+    return jnp.concatenate(
+        [
+            jnp.concatenate([y[:SIZE, :SIZE], y[SIZE:, :SIZE]], axis=1),
+            jnp.concatenate([y[:SIZE, SIZE:], y[SIZE:, SIZE:]], axis=1),
+        ],
+        axis=0,
+    )
+
+
+def visit_kernel(with_weight, *refs):
+    unit = (2 * SIZE, 2 * SIZE)
+    accumulators = [pltpu.ACC(u)(unit, F32) for _ in range(4) for u in range(PAIR)]
+    pl.run_scoped(functools.partial(visit_slots, with_weight, refs), *accumulators)
+
+
+def visit_slots(with_weight, refs, *accumulators):
+    off, cnt, ext, probe, table, amp, tot, *refs = refs
     if with_weight:
-        tot, wgt, grad, spread = refs
+        wgt, *refs = refs
         wgt[...] = jnp.zeros_like(wgt)
-    else:
-        tot, grad, spread = refs
+    grad, spread, power, *pairs, kept = refs
+    exits, first, second, third = (tuple(pairs[i : i + 2]) for i in (0, 2, 4, 6))
+    acc_a, acc_b, acc_c, acc_d = (accumulators[i : i + PAIR] for i in range(0, 4 * PAIR, PAIR))
     tot[...] = jnp.zeros_like(tot)
     grad[...] = jnp.zeros_like(grad)
     spread[...] = jnp.zeros_like(spread)
-    count = cnt[0]
+    if with_weight:
+        power[...] = probe[0, 0] ** 2 + probe[0, 1] ** 2 + probe[1, 0] ** 2 + probe[1, 1] ** 2
+    count = cnt[0, 0]
+    slots = amp.shape[0]
     lane = lanes(SIZE)
-
-    def step(index, carry):
-        modes = [(probe[0, m], probe[1, m]) for m in range(2)]
-        power = modes[0][0] ** 2 + modes[0][1] ** 2 + modes[1][0] ** 2 + modes[1][1] ** 2
-        exits, states = [], []
-        for u in range(UNROLL):
-            slot = index * UNROLL + u
-            row = off[slot, 0] + HALF
-            col = off[slot, 1] + SIZE
-            panel, shift = col // SIZE, col % SIZE
-            live = (slot < count).astype(F32)
-            upper = lane >= shift
-            back = (SIZE - shift) % SIZE
-            window = []
-            for part in range(2):
-                first = ext[part, panel, pl.ds(row, SIZE), :]
-                second = ext[part, panel + 1, pl.ds(row, SIZE), :]
-                window.append(pltpu.roll(jnp.where(upper, first, second), back, 1))
-            squared = window[0] * window[0] + window[1] * window[1]
-            mean = jnp.sum(jnp.sum(squared, axis=0, keepdims=True), axis=1, keepdims=True) * (1.0 / SIZE**2) + EPSILON
-            scale = live / mean
-            spread[...] += squared * scale
-            real = jnp.concatenate([pr * window[0] - pi * window[1] for pr, pi in modes], axis=1)
-            imag = jnp.concatenate([pr * window[1] + pi * window[0] for pr, pi in modes], axis=1)
-            exits.append(jnp.concatenate([real, imag], axis=0))
-            states.append((slot, row, panel, shift, upper, live, window[0] * scale, window[1] * scale))
-        first = [on_rows(table, 1, x) for x in exits]
-        turned = jnp.concatenate(
-            [
-                jnp.concatenate([y[:SIZE, m * SIZE : (m + 1) * SIZE], y[SIZE:, m * SIZE : (m + 1) * SIZE]], axis=1)
-                for y in first
-                for m in range(2)
-            ],
-            axis=0,
-        )
-        spectrum = on_columns(turned, table, 0)
-        scaled = []
-        for u in range(UNROLL):
-            z = spectrum[u * 2 * SIZE : (u + 1) * 2 * SIZE]
-            sq = z * z
-            level = sq[:SIZE, :SIZE] + sq[:SIZE, SIZE:] + sq[SIZE:, :SIZE] + sq[SIZE:, SIZE:]
-            factor = amp[states[u][0]] * jnp.minimum(lax.rsqrt(level), 1.0)
-            both = jnp.concatenate([factor, factor], axis=1)
-            scaled += [z[:SIZE] * both, z[SIZE:] * both]
-        middle = on_columns(jnp.concatenate(scaled, axis=0), table, 1)
-        terms = [[0.0, 0.0], [0.0, 0.0]]
-        for u in range(UNROLL):
-            slot, row, panel, shift, upper, live, wr, wi = states[u]
-            q = middle[u * 2 * SIZE : (u + 1) * 2 * SIZE]
-            revised = on_rows(
-                table,
-                0,
-                jnp.concatenate(
-                    [
-                        jnp.concatenate([q[:SIZE, :SIZE], q[SIZE:, :SIZE]], axis=1),
-                        jnp.concatenate([q[:SIZE, SIZE:], q[SIZE:, SIZE:]], axis=1),
-                    ],
-                    axis=0,
-                ),
-            )
-            real, imag = 0.0, 0.0
-            for m in range(2):
-                vr = revised[:SIZE, m * SIZE : (m + 1) * SIZE]
-                vi = revised[SIZE:, m * SIZE : (m + 1) * SIZE]
-                pr, pi = modes[m]
-                real = real + (pr * vr + pi * vi)
-                imag = imag + (pr * vi - pi * vr)
-                terms[m][0] = terms[m][0] + (wr * vr + wi * vi)
-                terms[m][1] = terms[m][1] + (wr * vi - wi * vr)
-            places = [(tot.at[0], real), (tot.at[1], imag)]
-            if with_weight:
-                places.append((wgt, power))
-            for ref, value in places:
-                moved = pltpu.roll(value * live, shift, 1)
-                ref[panel, pl.ds(row, SIZE), :] += jnp.where(upper, moved, 0.0)
-                ref[panel + 1, pl.ds(row, SIZE), :] += jnp.where(upper, 0.0, moved)
+    both = range(PAIR)
+
+    def clamped(index, u):
+        return jnp.minimum(index * PAIR + u, slots - 1)
+
+    def live(index, u):
+        return (index * PAIR + u < count).astype(F32)
+
+    def corner(index, u):
+        slot = clamped(index, u)
+        row = off[0, slot] + HALF
+        col = off[1, slot] + SIZE
+        return row, col // SIZE, col % SIZE
+
+    def on_rows(acc, which, terms, u):
+        high, low = terms
+        pltpu.matmul_push_rhs(high[u], 0, u)
+        pltpu.matmul_push_rhs(low[u], 1, u)
+        pltpu.matmul_acc_lhs(acc[u], table[2 * which], load_staged_rhs=0)
+        pltpu.matmul_acc_lhs(acc[u], table[2 * which + 1])
+        pltpu.matmul_acc_lhs(acc[u], table[2 * which], load_staged_rhs=1)
+
+    def on_columns(acc, which, terms, u):
+        high, low = terms
+        pltpu.matmul_push_rhs(table[2 * which], 0, u)
+        pltpu.matmul_push_rhs(table[2 * which + 1], 1, u)
+        pltpu.matmul_acc_lhs(acc[u], high[u], load_staged_rhs=0)
+        pltpu.matmul_acc_lhs(acc[u], low[u])
+        pltpu.matmul_acc_lhs(acc[u], high[u], load_staged_rhs=1)
+
+    def keep_terms(terms, u, value):
+        terms[0][u], terms[1][u] = split(value)
+
+    def fetch(index, u):
+        row, panel, shift = corner(index, u)
+        upper = lane >= shift
+        back = (SIZE - shift) % SIZE
+        window = []
+        for part in range(2):
+            near = ext[part, panel, pl.ds(row, SIZE), :]
+            far = ext[part, panel + 1, pl.ds(row, SIZE), :]
+            window.append(pltpu.roll(jnp.where(upper, near, far), back, 1))
+        squared = window[0] * window[0] + window[1] * window[1]
+        mean = jnp.sum(jnp.sum(squared, axis=0, keepdims=True), axis=1, keepdims=True) * (1.0 / SIZE**2) + EPSILON
+        scale = live(index, u) / mean
+        for m in range(2):
+            pr, pi = probe[0, m], probe[1, m]
+            block = pl.ds(m * SIZE, SIZE)
+            for rows, value in (
+                (pl.ds(0, SIZE), pr * window[0] - pi * window[1]),
+                (pl.ds(SIZE, SIZE), pr * window[1] + pi * window[0]),
+            ):
+                high, low = split(value)
+                exits[0][u, rows, block] = high
+                exits[1][u, rows, block] = low
+        place = index % 3
+        kept[place, u, 0] = window[0] * scale
+        kept[place, u, 1] = window[1] * scale
+        spread[...] += squared * scale
+
+    def rescale(index, u):
+        z = pltpu.matmul_pop(acc_b[u])
+        sq = z * z
+        level = sq[:SIZE, :SIZE] + sq[:SIZE, SIZE:] + sq[SIZE:, :SIZE] + sq[SIZE:, SIZE:]
+        factor = amp[clamped(index, u)] * (jnp.minimum(lax.rsqrt(level), 1.0) * live(index, u))
+        wide = jnp.concatenate([factor, factor], axis=1)
+        keep_terms(second, u, jnp.concatenate([z[:SIZE] * wide, z[SIZE:] * wide], axis=0))
+
+    def place(index, u):
+        row, panel, shift = corner(index, u)
+        upper = lane >= shift
+        revised = pltpu.matmul_pop(acc_d[u])
+        wr, wi = kept[index % 3, u, 0], kept[index % 3, u, 1]
+        real, imag, terms = 0.0, 0.0, []
+        for m in range(2):
+            vr = revised[:SIZE, m * SIZE : (m + 1) * SIZE]
+            vi = revised[SIZE:, m * SIZE : (m + 1) * SIZE]
+            pr, pi = probe[0, m], probe[1, m]
+            real = real + (pr * vr + pi * vi)
+            imag = imag + (pr * vi - pi * vr)
+            terms.append((wr * vr + wi * vi, wr * vi - wi * vr))
+        add_at(tot.at[0], row, panel, shift, upper, real)
+        add_at(tot.at[1], row, panel, shift, upper, imag)
+        return terms
+
+    def add_at(ref, row, panel, shift, upper, value):
+        moved = pltpu.roll(value, shift, 1)
+        near, far = ref.at[panel, pl.ds(row, SIZE), :], ref.at[panel + 1, pl.ds(row, SIZE), :]
+        pltpu.store(near, near[...] + moved, mask=upper)
+        pltpu.store(far, far[...] + moved, mask=jnp.logical_not(upper))
+
+    def weigh(index, u):
+        if with_weight:
+            row, panel, shift = corner(index, u)
+            add_at(wgt, row, panel, shift, lane >= shift, power[...] * live(index, u))
+
+    def add_terms(terms):
         for m in range(2):
             for part in range(2):
-                grad[part, m] += terms[m][part]
+                grad[part, m] += terms[0][m][part] + terms[1][m][part]
+
+    pairs_live = (count + PAIR - 1) // PAIR
+    for u in both:
+        fetch(0, u)
+    for u in both:
+        on_rows(acc_a, 1, exits, u)
+    for u in both:
+        fetch(1, u)
+    for u in both:
+        keep_terms(first, u, turned(pltpu.matmul_pop(acc_a[u])))
+    for u in both:
+        on_columns(acc_b, 0, first, u)
+    for u in both:
+        on_rows(acc_a, 1, exits, u)
+    for u in both:
+        weigh(0, u)
+    for u in both:
+        rescale(0, u)
+
+    def slotwise(index, carry):
+        terms = []
+        for u in both:
+            keep_terms(first, u, turned(pltpu.matmul_pop(acc_a[u])))
+            on_columns(acc_c, 1, second, u)
+            fetch(index + 1, u)
+            on_columns(acc_b, 0, first, u)
+            keep_terms(third, u, turned(pltpu.matmul_pop(acc_c[u])))
+            on_rows(acc_d, 0, third, u)
+            weigh(index, u)
+            rescale(index, u)
+            on_rows(acc_a, 1, exits, u)
+            terms.append(place(index - 1, u))
+        add_terms(terms)
         return carry
 
-    lax.fori_loop(0, (count + UNROLL - 1) // UNROLL, step, 0)
+    def pairwise(index, carry):
+        for u in both:
+            keep_terms(first, u, turned(pltpu.matmul_pop(acc_a[u])))
+        for u in both:
+            on_columns(acc_c, 1, second, u)
+        fetch(index + 1, 0)
+        for u in both:
+            keep_terms(third, u, turned(pltpu.matmul_pop(acc_c[u])))
+        for u in both:
+            on_columns(acc_b, 0, first, u)
+        fetch(index + 1, 1)
+        for u in both:
+            rescale(index, u)
+        for u in both:
+            on_rows(acc_d, 0, third, u)
+        terms = [place(index - 1, u) for u in both]
+        for u in both:
+            on_rows(acc_a, 1, exits, u)
+        add_terms(terms)
+        return carry
+
+    lax.fori_loop(1, pairs_live, slotwise if with_weight else pairwise, 0)
+    for u in both:
+        on_columns(acc_c, 1, second, u)
+    for u in both:
+        keep_terms(third, u, turned(pltpu.matmul_pop(acc_c[u])))
+    for u in both:
+        on_rows(acc_d, 0, third, u)
+    add_terms([place(pairs_live - 1, u) for u in both])
+    for u in both:
+        keep_terms(first, u, pltpu.matmul_pop(acc_a[u]))
     for part in range(2):
         for m in range(2):
             grad[part, m] -= probe[part, m] * spread[...]
@@ -525,45 +648,49 @@
         out_shape=outs,
         in_specs=[SMEM, SMEM, VMEM, VMEM, VMEM, VMEM],
         out_specs=[VMEM] * len(outs),
-        scratch_shapes=[pltpu.VMEM((SIZE, SIZE), F32)],
+        scratch_shapes=[pltpu.VMEM((SIZE, SIZE), F32)] * 2
+        + [pltpu.VMEM((PAIR, 2 * SIZE, 2 * SIZE), BF16)] * 8
+        + [pltpu.VMEM((3, PAIR, 2, SIZE, SIZE), F32)],
         compiler_params=pltpu.CompilerParams(vmem_limit_bytes=32 << 20),
         name="visit",
     )(off, cnt, ext, probe, table, amp)
 
 
-def remote_call(kernel, name, collective_id, outs, scratch, *args):
+def remote_call(kernel, name, collective_id, outs, scratch, *args, specs=None, cost=None):
     return pl.pallas_call(
         kernel,
         out_shape=outs,
-        in_specs=[VMEM] * len(args),
+        in_specs=specs or [VMEM] * len(args),
         out_specs=jax.tree.map(lambda _: VMEM, outs),
         scratch_shapes=scratch,
         compiler_params=pltpu.CompilerParams(
             collective_id=collective_id, has_side_effects=True, vmem_limit_bytes=32 << 20
         ),
+        cost_estimate=cost,
         name=name,
     )(*args)
 
 
 def local(field, probe, amplitudes, offsets, counts):
     amp = amplitudes[0, 0]
-    off = offsets[0, 0]
-    cnt = counts[0]
+    offsets = offsets[0, 0].T
     table = jnp.asarray(dft_tables())
     buffer = pltpu.VMEM((TILE, SIZE), F32)
     long = pltpu.VMEM((EXT, SIZE), F32)
     own = pltpu.VMEM((2, 2, TILE, SIZE), F32)
     ext = remote_call(
-        margins_kernel, "margins", 0, shape(2, 4, EXT, SIZE), FIELD_SCRATCH + [own, buffer, buffer], field
+        margins_kernel, "margins", 0, shape(2, 4, EXT, SIZE),
+        FIELD_SCRATCH + [own, buffer, buffer, pltpu.SemaphoreType.DMA((4,))],
+        field, specs=[pl.BlockSpec(memory_space=pltpu.HBM)], cost=pl.CostEstimate(flops=10**10, bytes_accessed=10**7, transcendentals=0),
     )
-    tot, wgt, grad_a = visit(True, off, cnt, ext, probe, table, amp)
+    tot, wgt, grad_a = visit(True, offsets, counts, ext, probe, table, amp)
     packed = pltpu.VMEM((SIZE, SIZE), F32)
     ext, den = remote_call(
         middle_kernel, "middle", 1, [shape(2, 4, EXT, SIZE), shape(2, TILE, SIZE)],
         FIELD_SCRATCH + WEIGHT_SCRATCH + FIELD_SCRATCH + [long, long, packed, packed, own, buffer, buffer],
         tot, wgt, ext, probe,
     )
-    tot, grad_b = visit(False, off, cnt, ext, probe, table, amp)
+    tot, grad_b = visit(False, offsets, counts, ext, probe, table, amp)
     plane, line = XS * YS, ZS
     dma = pltpu.SemaphoreType.DMA
     scratch = FIELD_SCRATCH + [
@@ -575,7 +702,7 @@
         pltpu.VMEM((SHARE, SIZE), F32),
         pltpu.VMEM((line, SHARE, SIZE), F32),
         pltpu.VMEM((4 * SIZE, SIZE), F32),
-        dma, dma, dma((plane,)), dma((plane,)), dma((line,)), dma((line,)), dma((plane,)), dma((plane,)), dma, dma,
+        *[dma((n,)) for n in (plane, plane, plane, plane, line, line, plane, plane, plane, plane)],
     ]
     field_new, probe_new = remote_call(
         last_kernel, "last", 2, [shape(2, TILE, TILE), shape(4 * SIZE, SIZE)], scratch,

time: 98.1 us -> 91.4 us (0.932); the launches traced: 99.1 us -> 90.7 us
  Pallas kernels: 93.2 us -> 86.8 us
  local copies, waits for them, and re-layouts: 4.35 us -> 2.55 us
    pallas_call x2, Pallas kernels: 13.9 us -> 5.88 us  [visit(): pl.pallas_call(functools.partial(visit_kernel, with_weight), out_shape=ou...]
    pallas_call x3, Pallas kernels: 79.3 us -> 80.9 us  [remote_call(): pl.pallas_call(kernel, out_shape=outs, in_specs=specs or [VMEM] * len(arg...]
    unnamed x12, local copies, waits for them, and re-layouts: 3.59 us -> 2.55 us
where the time goes in v1:
time: 91.4 us; the launch traced here: 90.7 us
  Pallas kernels  86.8 us (95%)
  local copies, waits for them, and re-layouts  2.55 us (3%)
  between operations  1.36 us (1%)
    pallas_call x3, Pallas kernels, remote_call(): pl.pallas_call(kernel, out_shape=outs, in_specs=specs or [VMEM] * len(arg...  80.9 us
    pallas_call x2, Pallas kernels, visit(): pl.pallas_call(functools.partial(visit_kernel, with_weight), out_shape=ou...  5.88 us
    unnamed x12, local copies, waits for them, and re-layouts  2.55 us

profile of v1, /device:TPU:1, one launch (start us, length us, event | category | flops | bytes accessed | tf_op | source)
XLA Modules:
  0.0 90.7 jit_solution(1593822388428573041)
XLA Ops:
  1.3 0.0 copy-start.4
  1.3 1.0 %copy-done.4 = f32[2,256,256]{2,1,0:T(8,128)S(1)} copy-done((f32[2,256,256]{2,1,0:T(8,128)S(1)}, f32[2,256,256]{2,1,0:T(8,128)}, u32[]{:S(2)}) %copy-start.4) | copy-done | bytes 524312
  2.3 0.0 copy-start
  2.3 0.0 copy-start.1
  2.3 0.0 copy-start.2
  2.3 0.0 copy-start.3
  2.3 10.8 %margins.1.refs_2_.ext = f32[2,4,384,128]{3,2,1,0:T(8,128)S(1)} custom-call(f32[2,256,256]{2,1,0:T(8,128)S(1)} %copy-done.4), custom_call_target="tpu_custom_call" | custom-call | flops 10000000000 | bytes 10000000 | tf_op jit(solution)/shard_map/margins/pallas_call | solution.py:660
  13.2 0.0 copy-done
  13.2 0.0 copy-done.1
  13.2 0.0 copy-done.2
  13.2 0.0 copy-done.3
  13.2 3.0 %visit.2 = (f32[2,4,384,128]{3,2,1,0:T(8,128)S(1)}, f32[4,384,128]{2,1,0:T(8,128)S(1)}, f32[2,2,128,128]{3,2,1,0:T(8,128)S(1)}) custom-call(s32[2,24]{1,0:T(2,128)S(1)} %bitcast.10, s32[1,1]{1,0:T(1,128)S(6)} %copy.10.refs_1_, f32[2,4,384,128]{3,2,1,0:T(8,128)S(1)} %margins.1.refs_2_.ext, f32[2,2,128,128]{3,2,1,0:T(8,128)S(1)} %copy-done.1, ...), custom_call_target="tpu_custom_call" | custom-call | tf_op jit(solution)/shard_map/visit/pallas_call | solution.py:646
  16.2 23.0 %middle.1 = (f32[2,4,384,128]{3,2,1,0:T(8,128)S(1)}, f32[2,256,128]{2,1,0:T(8,128)S(1)}) custom-call(f32[2,4,384,128]{3,2,1,0:T(8,128)S(1)} %get-tuple-element.11.tot, f32[4,384,128]{2,1,0:T(8,128)S(1)} %get-tuple-element.12.wgt, f32[2,4,384,128]{3,2,1,0:T(8,128)S(1)} %margins.1.refs_2_.ext, f32[2,2,128,128]{3,2,1,0:T(8,128)S(1)} %copy-done.1), custom_call_target="tpu_custom_call" | custom-call | tf_op jit(solution)/shard_map/middle/pallas_call | solution.py:660
  39.2 2.9 %visit.3 = (f32[2,4,384,128]{3,2,1,0:T(8,128)S(1)}, f32[2,2,128,128]{3,2,1,0:T(8,128)S(1)}) custom-call(s32[2,24]{1,0:T(2,128)S(1)} %bitcast.11, s32[1,1]{1,0:T(1,128)S(6)} %copy.10.refs_1_, f32[2,4,384,128]{3,2,1,0:T(8,128)S(1)} %get-tuple-element.13.refs_2_.ext, f32[2,2,128,128]{3,2,1,0:T(8,128)S(1)} %copy-done.1, bf16[4,256,256]{2,1,0:T(8,128)(2,1)S(1)} %copy-done.2, ...), custom_call_target="tpu_custom_call" | custom-call | tf_op jit(solution)/shard_map/visit/pallas_call | solution.py:646
  42.1 47.1 %last.1 = (f32[2,256,256]{2,1,0:T(8,128)S(1)}, f32[512,128]{1,0:T(8,128)S(1)}) custom-call(f32[2,4,384,128]{3,2,1,0:T(8,128)S(1)} %get-tuple-element.14.tot, f32[2,256,128]{2,1,0:T(8,128)S(1)} %get-tuple-element.15.den, f32[2,4,384,128]{3,2,1,0:T(8,128)S(1)} %get-tuple-element.13.refs_2_.ext, f32[512,128]{1,0:T(8,128)S(1)} %bitcast.8, ...), custom_call_target="tpu_custom_call" | custom-call | tf_op jit(solution)/shard_map/last/pallas_call | solution.py:660
  89.2 0.8 copy.11
  90.0 0.7 copy.12
Async XLA Ops:
  1.3 1.0 %copy-start.4 = (f32[2,256,256]{2,1,0:T(8,128)S(1)}, f32[2,256,256]{2,1,0:T(8,128)}, u32[]{:S(2)}) copy-start(f32[2,256,256]{2,1,0:T(8,128)} %field.1) | copy-start | bytes 1572868
  2.3 10.8 %copy-start = (f32[1,1,24,128,128]{4,3,2,1,0:T(8,128)S(1)}, f32[1,1,24,128,128]{4,3,2,1,0:T(8,128)}, u32[]{:S(2)}) copy-start(f32[1,1,24,128,128]{4,3,2,1,0:T(8,128)} %param.8) | copy-start | bytes 4718596
  2.3 10.9 %copy-start.1 = (f32[2,2,128,128]{3,2,1,0:T(8,128)S(1)}, f32[2,2,128,128]{3,2,1,0:T(8,128)}, u32[]{:S(2)}) copy-start(f32[2,2,128,128]{3,2,1,0:T(8,128)} %refs_3_.3) | copy-start | bytes 786436
  2.3 10.9 %copy-start.2 = (bf16[4,256,256]{2,1,0:T(8,128)(2,1)S(1)}, bf16[4,256,256]{2,1,0:T(8,128)(2,1)}, u32[]{:S(2)}) copy-start(bf16[4,256,256]{2,1,0:T(8,128)(2,1)} %constant.2.clone.refs_4_) | copy-start | bytes 1572868
  2.3 10.9 %copy-start.3 = (s32[1,1,24,2]{2,3,1,0:T(2,128)S(1)}, s32[1,1,24,2]{2,3,1,0:T(2,128)}, u32[]{:S(2)}) copy-start(s32[1,1,24,2]{2,3,1,0:T(2,128)} %param.9) | copy-start | bytes 580

commit v2 on v1

--- a/solution.py
+++ b/solution.py
@@ -293,6 +293,9 @@
         margins.wait_send(k, srcs[k])
 
 
+FAR_FIRST = sorted(
+    range(XS * YS), key=lambda d: -(min(d // YS, XS - d // YS) + min(d % YS, YS - d % YS))
+)
 SHARE = 4 * SIZE // (2 * XS * YS)
 
 
@@ -306,9 +309,15 @@
     x, z = col // ZS, col % ZS
     place = x * YS + y
 
+    def plane_place(step_x, step_y):
+        return (x + step_x + XS) % XS * YS + (y + step_y + YS) % YS
+
     def in_plane(d):
-        other = (place + d) % (XS * YS)
+        other = plane_place(d // YS, d % YS)
         return other, ((other % YS) * 2 + core, (other // YS) * ZS + z)
+
+    def source_in_plane(d):
+        return plane_place(-(d // YS), -(d % YS))
 
     def in_line(d):
         other = (z + d) % ZS
@@ -344,8 +353,7 @@
     def swap_copy(d):
         return remote(total.at[share_of(theirs, d)], from_core.at[share_of(0, d)], core_send.at[d], core_recv.at[d], partner)
 
-    order = list(range(1, XS * YS)) + [0]
-    for d in order:
+    for d in FAR_FIRST:
         swap_copy(d).start()
     tot_srcs = send_totals(totals, tot, tot_left, tot_right)
 
@@ -353,12 +361,29 @@
         _, where = in_plane(d)
         return remote(half.at[share_of(0, d)], from_plane.at[d], plane_send.at[d], plane_recv.at[d], where)
 
-    for d in order:
+    for d in FAR_FIRST:
         swap_copy(d).wait_recv()
         half[share_of(0, d), :] = total[share_of(mine, d), :] + from_core[share_of(0, d), :]
         if d:
             plane_copy(d).start()
 
+    share = half[pl.ds(pl.multiple_of(place * SHARE, SHARE), SHARE), :]
+    for d in FAR_FIRST[-2::-1]:
+        plane_copy(d).wait_recv()
+        share = share + from_plane[d]
+    piece[...] = share
+    from_line[z] = share
+
+    def line_copy(d):
+        _, where = in_line(d)
+        return remote(piece, from_line.at[z], line_send.at[d], line_recv.at[d], where)
+
+    def line_arrival(d):
+        source = (z - d + ZS) % ZS
+        return remote(piece, from_line.at[source], line_send.at[d], line_recv.at[d], in_line(d)[1])
+
+    for d in range(1, ZS):
+        line_copy(d).start()
     numer = gathered_totals(totals, tot)
     power = probe[0:SIZE] ** 2
     for k in range(1, 4):
@@ -368,24 +393,6 @@
         for panel in range(2):
             own = ext[part, 1 + panel, pl.ds(HALF, TILE), :]
             field[part, :, panel * SIZE : (panel + 1) * SIZE] = (numer[part][panel] + regular * own) / den[panel]
-
-    share = half[pl.ds(pl.multiple_of(place * SHARE, SHARE), SHARE), :]
-    for d in range(1, XS * YS):
-        plane_copy(d).wait_recv()
-        share = share + from_plane[d]
-    piece[...] = share
-    from_line[z] = share
-
-    def line_copy(d):
-        _, where = in_line(d)
-        return remote(piece, from_line.at[z], line_send.at[d], line_recv.at[d], where)
-
-    def line_arrival(d):
-        source = (z - d + ZS) % ZS
-        return remote(piece, from_line.at[source], line_send.at[d], line_recv.at[d], in_line(d)[1])
-
-    for d in range(1, ZS):
-        line_copy(d).start()
     for d in range(1, ZS):
         line_arrival(d).wait_recv()
     summed = from_line[0]
@@ -400,18 +407,17 @@
         return remote(fresh.at[rows], fresh.at[rows], spread_send.at[d], spread_recv.at[d], where)
 
     def spread_arrival(d):
-        source = (place - d + XS * YS) % (XS * YS)
-        there = pl.ds(pl.multiple_of(mine + source * SHARE, SHARE), SHARE)
+        there = pl.ds(pl.multiple_of(mine + source_in_plane(d) * SHARE, SHARE), SHARE)
         return remote(fresh.at[rows], fresh.at[there], spread_send.at[d], spread_recv.at[d], in_plane(d)[1])
 
     def back_copy(d, start):
-        there = pl.ds(pl.multiple_of(start + (place - d + XS * YS) % (XS * YS) * SHARE, SHARE), SHARE)
+        there = pl.ds(pl.multiple_of(start + source_in_plane(d) * SHARE, SHARE), SHARE)
         return remote(fresh.at[there], fresh.at[there], back_send.at[d], back_recv.at[d], partner)
 
-    for d in range(1, XS * YS):
+    for d in FAR_FIRST[:-1]:
         spread_copy(d).start()
     back_copy(0, mine).start()
-    for d in range(1, XS * YS):
+    for d in FAR_FIRST[-2::-1]:
         spread_arrival(d).wait_recv()
         back_copy(d, mine).start()
     for d in range(XS * YS):
@@ -637,6 +643,31 @@
             grad[part, m] -= probe[part, m] * spread[...]
 
 
+def store_kernel(field, probe, field_out, probe_out, done):
+    copies = [
+        pltpu.make_async_copy(field.at[0], field_out.at[0], done.at[0]),
+        pltpu.make_async_copy(field.at[1], field_out.at[1], done.at[1]),
+        pltpu.make_async_copy(probe, probe_out, done.at[2]),
+    ]
+    for copy in copies:
+        copy.start()
+    for copy in copies:
+        copy.wait()
+
+
+def store(field, probe):
+    hbm = pl.BlockSpec(memory_space=pltpu.HBM)
+    return pl.pallas_call(
+        store_kernel,
+        out_shape=[shape(*field.shape), shape(*probe.shape)],
+        in_specs=[VMEM, VMEM],
+        out_specs=[hbm, hbm],
+        scratch_shapes=[pltpu.SemaphoreType.DMA((3,))],
+        compiler_params=pltpu.CompilerParams(vmem_limit_bytes=32 << 20),
+        name="store",
+    )(field, probe)
+
+
 def shape(*dims):
     return jax.ShapeDtypeStruct(dims, F32)
 
@@ -681,7 +712,7 @@
     ext = remote_call(
         margins_kernel, "margins", 0, shape(2, 4, EXT, SIZE),
         FIELD_SCRATCH + [own, buffer, buffer, pltpu.SemaphoreType.DMA((4,))],
-        field, specs=[pl.BlockSpec(memory_space=pltpu.HBM)], cost=pl.CostEstimate(flops=10**10, bytes_accessed=10**7, transcendentals=0),
+        pltpu.with_memory_space_constraint(field, pltpu.HBM), specs=[pl.BlockSpec(memory_space=pltpu.HBM)], cost=pl.CostEstimate(flops=10**10, bytes_accessed=10**7, transcendentals=0),
     )
     tot, wgt, grad_a = visit(True, offsets, counts, ext, probe, table, amp)
     packed = pltpu.VMEM((SIZE, SIZE), F32)
@@ -708,7 +739,7 @@
         last_kernel, "last", 2, [shape(2, TILE, TILE), shape(4 * SIZE, SIZE)], scratch,
         tot, den, ext, probe.reshape(4 * SIZE, SIZE), grad_a, grad_b,
     )
-    return field_new, probe_new.reshape(2, 2, SIZE, SIZE)
+    return store(field_new, probe_new.reshape(2, 2, SIZE, SIZE))
 
 
 def solution(mesh):

time: 91.4 us -> 89.6 us (0.980)
  local copies, waits for them, and re-layouts: 2.55 us -> 0.02 us
  Pallas kernels: 86.8 us -> 88.1 us
    pallas_call x2, Pallas kernels: 5.88 us -> 10.9 us  [visit(): pl.pallas_call(functools.partial(visit_kernel, with_weight), out_shape=ou...]
    pallas_call x3, Pallas kernels: 80.9 us -> 76.3 us  [remote_call(): pl.pallas_call(kernel, out_shape=outs, in_specs=specs or [VMEM] * len(arg...]
    unnamed x12 -> x8, local copies, waits for them, and re-layouts: 2.55 us -> 0.02 us
where the time goes in v2:
time: 89.6 us; the launch traced here: 89.5 us
  Pallas kernels  88.1 us (98%)
  between operations  1.38 us (2%)
    pallas_call x3, Pallas kernels, remote_call(): pl.pallas_call(kernel, out_shape=outs, in_specs=specs or [VMEM] * len(arg...  76.3 us
    pallas_call x2, Pallas kernels, visit(): pl.pallas_call(functools.partial(visit_kernel, with_weight), out_shape=ou...  10.9 us

profile of v2, /device:TPU:1, one launch (start us, length us, event | category | flops | bytes accessed | tf_op | source)
XLA Modules:
  0.0 89.5 jit_solution(8928879157627685434)
XLA Ops:
  1.3 0.0 copy-start
  1.3 0.0 copy-start.1
  1.3 0.0 copy-start.2
  1.3 0.0 copy-start.3
  1.3 10.8 %margins.1.refs_2_.ext = f32[2,4,384,128]{3,2,1,0:T(8,128)S(1)} custom-call(f32[2,256,256]{2,1,0:T(8,128)} %field.1), custom_call_target="tpu_custom_call" | custom-call | flops 10000000000 | bytes 10000000 | tf_op jit(solution)/shard_map/margins/pallas_call | solution.py:691
  12.1 0.0 copy-done
  12.1 0.0 copy-done.1
  12.1 0.0 copy-done.2
  12.1 0.0 copy-done.3
  12.2 5.6 %visit.2 = (f32[2,4,384,128]{3,2,1,0:T(8,128)S(1)}, f32[4,384,128]{2,1,0:T(8,128)S(1)}, f32[2,2,128,128]{3,2,1,0:T(8,128)S(1)}) custom-call(s32[2,24]{1,0:T(2,128)S(1)} %bitcast.10, s32[1,1]{1,0:T(1,128)S(6)} %copy.8.refs_1_, f32[2,4,384,128]{3,2,1,0:T(8,128)S(1)} %margins.1.refs_2_.ext, f32[2,2,128,128]{3,2,1,0:T(8,128)S(1)} %copy-done.1, ...), custom_call_target="tpu_custom_call" | custom-call | tf_op jit(solution)/shard_map/visit/pallas_call | solution.py:677
  17.8 21.9 %middle.1 = (f32[2,4,384,128]{3,2,1,0:T(8,128)S(1)}, f32[2,256,128]{2,1,0:T(8,128)S(1)}) custom-call(f32[2,4,384,128]{3,2,1,0:T(8,128)S(1)} %get-tuple-element.11.tot, f32[4,384,128]{2,1,0:T(8,128)S(1)} %get-tuple-element.12.wgt, f32[2,4,384,128]{3,2,1,0:T(8,128)S(1)} %margins.1.refs_2_.ext, f32[2,2,128,128]{3,2,1,0:T(8,128)S(1)} %copy-done.1), custom_call_target="tpu_custom_call" | custom-call | tf_op jit(solution)/shard_map/middle/pallas_call | solution.py:691
  39.7 5.3 %visit.3 = (f32[2,4,384,128]{3,2,1,0:T(8,128)S(1)}, f32[2,2,128,128]{3,2,1,0:T(8,128)S(1)}) custom-call(s32[2,24]{1,0:T(2,128)S(1)} %bitcast.11, s32[1,1]{1,0:T(1,128)S(6)} %copy.8.refs_1_, f32[2,4,384,128]{3,2,1,0:T(8,128)S(1)} %get-tuple-element.13.refs_2_.ext, f32[2,2,128,128]{3,2,1,0:T(8,128)S(1)} %copy-done.1, bf16[4,256,256]{2,1,0:T(8,128)(2,1)S(1)} %copy-done.2, ...), custom_call_target="tpu_custom_call" | custom-call | tf_op jit(solution)/shard_map/visit/pallas_call | solution.py:677
  45.0 43.6 %last.1 = (f32[2,256,256]{2,1,0:T(8,128)S(1)}, f32[512,128]{1,0:T(8,128)S(1)}) custom-call(f32[2,4,384,128]{3,2,1,0:T(8,128)S(1)} %get-tuple-element.14.tot, f32[2,256,128]{2,1,0:T(8,128)S(1)} %get-tuple-element.15.den, f32[2,4,384,128]{3,2,1,0:T(8,128)S(1)} %get-tuple-element.13.refs_2_.ext, f32[512,128]{1,0:T(8,128)S(1)} %bitcast.8, ...), custom_call_target="tpu_custom_call" | custom-call | tf_op jit(solution)/shard_map/last/pallas_call | solution.py:691
  88.6 0.9 %store.1 = (f32[2,256,256]{2,1,0:T(8,128)}, f32[2,2,128,128]{3,2,1,0:T(8,128)}) custom-call(f32[2,256,256]{2,1,0:T(8,128)S(1)} %get-tuple-element.18.field, f32[2,2,128,128]{3,2,1,0:T(8,128)S(1)} %bitcast.9), custom_call_target="tpu_custom_call" | custom-call | tf_op jit(solution)/shard_map/store/pallas_call | solution.py:660
Async XLA Ops:
  1.3 10.8 %copy-start = (f32[1,1,24,128,128]{4,3,2,1,0:T(8,128)S(1)}, f32[1,1,24,128,128]{4,3,2,1,0:T(8,128)}, u32[]{:S(2)}) copy-start(f32[1,1,24,128,128]{4,3,2,1,0:T(8,128)} %param.8) | copy-start | bytes 4718596
  1.3 10.8 %copy-start.1 = (f32[2,2,128,128]{3,2,1,0:T(8,128)S(1)}, f32[2,2,128,128]{3,2,1,0:T(8,128)}, u32[]{:S(2)}) copy-start(f32[2,2,128,128]{3,2,1,0:T(8,128)} %refs_3_.3) | copy-start | bytes 786436
  1.3 10.8 %copy-start.2 = (bf16[4,256,256]{2,1,0:T(8,128)(2,1)S(1)}, bf16[4,256,256]{2,1,0:T(8,128)(2,1)}, u32[]{:S(2)}) copy-start(bf16[4,256,256]{2,1,0:T(8,128)(2,1)} %constant.2.clone.refs_4_) | copy-start | bytes 1572868
  1.3 10.8 %copy-start.3 = (s32[1,1,24,2]{2,3,1,0:T(2,128)S(1)}, s32[1,1,24,2]{2,3,1,0:T(2,128)}, u32[]{:S(2)}) copy-start(s32[1,1,24,2]{2,3,1,0:T(2,128)} %param.9) | copy-start | bytes 580
